TPU v7x, 512 devices: a whole 4x8x8 slice. The times are simulated.
512 devices in a mesh: req: 128 (over y, z, core), tp: 4 (over x).
Axes of the slice: x: 4, y: 8, z: 8, core: 2. Of those that a mesh axis runs over, the one named last changes fastest.
Arguments:
- attn_out: bfloat16 [8192, 2048], P('req', 'tp'), may hold values from -6 to 6
- w_out: bfloat16 [2048, 2048], P('tp'), may hold values from -0.125 to 0.125
- residual: bfloat16 [8192, 2048], P('req', 'tp'), may hold values from -6 to 6
- routes: int32 [8192, 6], P('req'), may hold values from 0 to 127, all different within a row; in each aligned block of 64 rows (0 to 63, 64 to 127, ...) at most 6 rows name the same one
- gates: float32 [8192, 6], P('req'), may hold values from 0.05 to 1
- w_gate: bfloat16 [128, 2048, 1024], P('req', None, 'tp'), as said below
- w_up: bfloat16 [128, 2048, 1024], P('req', None, 'tp'), as said below
- w_down: bfloat16 [128, 1024, 2048], P('req', None, 'tp'), as said below
- norm_gain: float32 [2048], P('tp'), may hold values from 0.1 to 1.9
Outputs:
- normed: bfloat16 [8192, 2048], P('req', 'tp')
Inputs may be any that keep to these rules, and one draw needn't show every extreme that they name: `routes`: each row names 6 different slots. In the 64 rows of one index of req no slot is named by more than 6 rows, a bound that some block reaches. `w_gate`: slots 2 e and 2 e + 1 hold the same expert e: their weights are equal. `w_up`: slots 2 e and 2 e + 1 hold the same expert e: their weights are equal. `w_down`: slots 2 e and 2 e + 1 hold the same expert e: their weights are equal.
All inputs are finite; a program needn't handle non-finite values.
Results may differ from a plain program's by a relative error of at most 0.0056.
Values may be sent and summed in bfloat16 or wider, within the bound.
A program may use at most 64 MiB of HBM per device.

v0:
```python
import jax
import jax.numpy as jnp
from jax import lax
from jax.sharding import PartitionSpec as P


def body(attn_out, w_out, residual, routes, gates, w_gate, w_up, w_down, norm_gain):
    row_count = attn_out.shape[0]
    part_width = residual.shape[1]
    full_width = w_out.shape[1]
    route_count = routes.shape[1]
    slot_count = lax.axis_size("req")
    capacity = max(2, min(row_count, 2 * row_count * route_count // slot_count))
    tp_index = lax.axis_index("tp")
    partial_value = jnp.dot(attn_out, w_out, preferred_element_type=jnp.float32)
    own_block = lax.dynamic_slice_in_dim(partial_value, tp_index * part_width, part_width, 1)
    partial_value = lax.dynamic_update_slice_in_dim(
        partial_value, own_block + residual.astype(jnp.float32), tp_index * part_width, 1
    )
    flat_routes = routes.reshape(-1)
    one_hot = (flat_routes[:, None] == jnp.arange(slot_count, dtype=jnp.int32)[None, :]).astype(
        jnp.int32
    )
    position = jnp.sum(one_hot * (jnp.cumsum(one_hot, axis=0) - 1), axis=1)
    dest_index = flat_routes * capacity + position
    row_ids = jnp.repeat(jnp.arange(row_count, dtype=jnp.int32), route_count)
    source_row = jnp.zeros((slot_count * capacity,), jnp.int32).at[dest_index].set(row_ids)
    gate_local = w_gate[0]
    up_local = w_up[0]
    down_local = w_down[0]
    projected = lax.psum(partial_value, "tp")
    own_part = lax.dynamic_slice_in_dim(projected, tp_index * part_width, part_width, 1)
    outgoing = projected.astype(jnp.bfloat16)[source_row].reshape(slot_count, capacity, full_width)
    incoming = lax.all_to_all(outgoing, "req", split_axis=0, concat_axis=0, tiled=True)
    expert_rows = incoming.reshape(slot_count * capacity, full_width)
    gate_act = jnp.dot(expert_rows, gate_local, preferred_element_type=jnp.float32)
    up_act = jnp.dot(expert_rows, up_local, preferred_element_type=jnp.float32)
    hidden = (jax.nn.silu(gate_act) * up_act).astype(jnp.bfloat16)
    expert_out = jnp.dot(
        lax.all_gather(hidden, "tp", axis=1, tiled=True),
        down_local,
        preferred_element_type=jnp.float32,
    )
    expert_out = expert_out.astype(jnp.bfloat16).reshape(slot_count, capacity, down_local.shape[1])
    returned = lax.all_to_all(expert_out, "req", split_axis=0, concat_axis=0, tiled=True)
    picked = returned.reshape(slot_count * capacity, part_width)[dest_index]
    picked = picked.reshape(row_count, route_count, part_width).astype(jnp.float32)
    routed_sum = jnp.sum(picked * gates[:, :, None], axis=1)
    combined = own_part + routed_sum
    square_part = jnp.sum(combined * combined, axis=1)
    square_total = lax.psum(square_part, "tp")
    scale = lax.rsqrt(square_total / full_width + 1e-06)
    return (combined * scale[:, None] * norm_gain[None, :]).astype(jnp.bfloat16)


def solution(mesh):
    placed = (
        P("req", "tp"),
        P("tp", None),
        P("req", "tp"),
        P("req", None),
        P("req", None),
        P("req", None, "tp"),
        P("req", None, "tp"),
        P("req", None, "tp"),
        P("tp"),
    )
    return jax.shard_map(
        body, mesh=mesh, in_specs=placed, out_specs=P("req", "tp"), check_vma=False
    )
```

profile of v0, /device:TPU:8, one launch (start us, length us, event | category | flops | bytes accessed | tf_op | source)
XLA Modules:
  0.0 315.9 jit_solution(1539475655118343820)
XLA Ops:
  6.5 0.0 copy-start
  6.5 0.0 copy-start.3
  6.5 0.0 all-reduce.2.cloned.1.call-start
  6.5 1.6 copy-done
  8.1 1.3 fusion.12
  9.4 0.9 add_dynamic-update-slice_fusion
  10.3 0.0 copy-start.2
  10.3 0.8 copy-done.2
  11.1 0.0 all-reduce.2.cloned.1.call-update
  11.1 0.0 all-gather.2.cloned.1.call-start
  11.2 0.0 copy-done.3
  11.2 0.1 copy.12
  11.3 0.1 eq.29
  11.4 0.1 eq.25
  11.6 0.1 copy.14
  11.7 0.2 fusion.5
  12.0 0.1 add_add_fusion
  12.0 0.1 copy.11
  12.1 0.1 mul.61
  12.3 0.1 reshape.96
  12.4 0.2 fusion.7
  12.7 2.9 scatter_custom_fusion
  15.6 53.9 %all-reduce.2.cloned.1.call-done = f32[64,2048]{1,0:T(8,128)} async-done(((f32[64,2048]{1,0:T(8,128)}), f32[64,2048]{1,0:T(8,128)}) %all-reduce.2.cloned.1.call-update) | async-done | bytes 524304 | tf_op jit(solution)/shard_map/psum | solution.py:31
  69.5 1.1 convert_element_type.27
  70.6 4.3 %gather_fusion = bf16[768,2048]{1,0:T(8,128)(2,1)} fusion(bf16[64,2048]{1,0:T(8,128)(2,1)S(1)} %convert_element_type.27, s32[1024]{0:T(1024)S(1)} %pad_clamp_fusion.1), kind=kCustom, calls=%fused_computation | custom fusion | bytes 6294528 | tf_op jit(solution)/shard_map/gather | solution.py:33
  74.9 6.3 %reshape.71 = bf16[128,6,2048]{2,1,0:T(8,128)(2,1)} reshape(bf16[768,2048]{1,0:T(8,128)(2,1)} %gather_fusion) | data formatting | bytes 6291456 | tf_op jit(solution)/shard_map/reshape | solution.py:33
  81.1 111.0 %all_to_all.10 = bf16[128,6,2048]{2,1,0:T(8,128)(2,1)} all-to-all(bf16[128,6,2048]{2,1,0:T(8,128)(2,1)} %reshape.71), channel_id=1, replica_groups=mesh['req'=128,'tp'=4] {'req'}, dimensions={0} | all-to-all | bytes 6291456 | tf_op jit(solution)/shard_map/all_to_all | solution.py:34
  192.1 6.3 %reshape.72 = bf16[768,2048]{1,0:T(8,128)(2,1)} reshape(bf16[128,6,2048]{2,1,0:T(8,128)(2,1)} %all_to_all.10) | data formatting | bytes 6291456 | tf_op jit(solution)/shard_map/reshape | solution.py:35
  198.4 0.0 copy-start.1
  198.4 0.0 copy-start.6
  198.4 3.3 %fusion.3 = f32[768,256]{1,0:T(8,128)S(1)} fusion(bf16[768,2048]{1,0:T(8,128)(2,1)} %reshape.72, bf16[1,2048,256]{2,1,0:T(8,128)(2,1)} %param.14), kind=kOutput, calls=%fused_computation.8 | convolution fusion | flops 805306368 | bytes 4980736 | tf_op jit(solution)/shard_map/dot_general | solution.py:36
  201.7 0.0 copy-done.1
  201.8 0.1 copy-done.6
  201.9 1.7 fusion
  203.6 0.0 all-gather.2.cloned.1.call-update
  203.6 38.7 %all-gather.2.cloned.1.call-done = bf16[768,1024]{1,0:T(8,128)(2,1)} async-done(((bf16[768,256]{1,0:T(8,128)(2,1)}), bf16[768,1024]{1,0:T(8,128)(2,1)}) %all-gather.2.cloned.1.call-update) | async-done | bytes 1572880 | tf_op jit(solution)/shard_map/all_gather | solution.py:40
  242.3 2.7 convolution_convert_fusion
  245.0 0.0 copy-start.4
  245.0 1.3 reshape.73
  246.3 14.6 %all-to-all-start.1 = ((bf16[128,6,512]{2,1,0:T(8,128)(2,1)}), bf16[128,6,512]{2,1,0:T(8,128)(2,1)}, u32[]{:S(2)}, u32[]{:S(2)}) async-start(bf16[128,6,512]{2,1,0:T(8,128)(2,1)} %reshape.73), calls=%async_computation.1 | async-start | bytes 2097152 | tf_op jit(solution)/shard_map/all_to_all | solution.py:45
  260.9 0.0 copy-done.4
  260.9 0.7 copy.16
  261.6 30.2 %all-to-all-done.1 = bf16[128,6,512]{2,1,0:T(8,128)(2,1)} async-done(((bf16[128,6,512]{2,1,0:T(8,128)(2,1)}), bf16[128,6,512]{2,1,0:T(8,128)(2,1)}, u32[]{:S(2)}, u32[]{:S(2)}) %all-to-all-start.1) | async-done | bytes 786464 | tf_op jit(solution)/shard_map/all_to_all | solution.py:45
  291.9 1.4 reshape.74
  293.2 0.0 copy-start.5
  293.3 2.1 gather_fusion.1
  295.3 0.1 reshape.75
  295.4 1.1 multiply_reduce_fusion
  296.6 1.0 multiply_reduce_fusion.1
  297.6 9.8 %psum.15 = f32[64]{0:T(128)S(1)} all-reduce(f32[64]{0:T(128)S(1)} %multiply_reduce_fusion.1), channel_id=1, replica_groups=mesh['req'=128,'tp'=4] {'tp'}, use_global_device_ids=true, to_apply=%region_7.8 | all-reduce | flops 64 | bytes 512 | tf_op jit(solution)/shard_map/psum | solution.py:51
  307.4 0.0 copy-done.5
  307.4 1.6 multiply_convert_fusion
  (10 shorter events, 0.1 us)
Async XLA Ops:
  6.5 1.6 copy-start
  6.5 4.6 %copy-start.3 = (s32[64,6]{0,1:T(8,128)S(1)}, s32[64,6]{0,1:T(8,128)}, u32[]{:S(2)}) copy-start(s32[64,6]{0,1:T(8,128)} %param.12) | copy-start | bytes 4612
  6.5 63.0 %all-reduce.2.cloned.1.call-start = ((), (), s32[]{:S(2)}) async-start(), calls=%async_computation.2 | async-start | bytes 1048576 | tf_op jit(solution)/shard_map/psum | solution.py:31
  10.3 0.8 copy-start.2
  11.1 231.1 %all-gather.2.cloned.1.call-start = ((), (), s32[]{:S(2)}) async-start(), calls=%async_computation.3 | async-start | bytes 1966080 | tf_op jit(solution)/shard_map/all_gather | solution.py:40
  198.4 3.3 %copy-start.1 = (bf16[768,2048]{1,0:T(8,128)(2,1)S(1)}, bf16[768,2048]{1,0:T(8,128)(2,1)}, u32[]{:S(2)}) copy-start(bf16[768,2048]{1,0:T(8,128)(2,1)} %reshape.72) | copy-start | bytes 9437188
  198.4 3.4 %copy-start.6 = (bf16[1,2048,256]{2,1,0:T(8,128)(2,1)S(1)}, bf16[1,2048,256]{2,1,0:T(8,128)(2,1)}, u32[]{:S(2)}) copy-start(bf16[1,2048,256]{2,1,0:T(8,128)(2,1)} %param.15) | copy-start | bytes 3145732
  245.0 15.9 %copy-start.4 = (f32[64,6]{0,1:T(8,128)S(1)}, f32[64,6]{0,1:T(8,128)}, u32[]{:S(2)}) copy-start(f32[64,6]{0,1:T(8,128)} %param.13) | copy-start | bytes 4612
  246.3 45.6 %all-to-all-start.1 = ((bf16[128,6,512]{2,1,0:T(8,128)(2,1)}), bf16[128,6,512]{2,1,0:T(8,128)(2,1)}, u32[]{:S(2)}, u32[]{:S(2)}) async-start(bf16[128,6,512]{2,1,0:T(8,128)(2,1)} %reshape.73), calls=%async_computation.1 | async-start | bytes 2097152 | tf_op jit(solution)/shard_map/all_to_all | solution.py:45
  293.2 14.2 %copy-start.5 = (f32[512]{0:T(512)S(1)}, f32[512]{0:T(512)}, u32[]{:S(2)}) copy-start(f32[512]{0:T(512)} %param.17) | copy-start | bytes 6148
Sparse Core Ops, SparseCore 0:
  11.3 58.2 all-reduce.1
  203.7 38.5 all-gather.1
where the time goes:
time: 317 us; the launch traced here: 316 us
  waiting for transfers between devices  123 us (39%)
  blocking collectives  121 us (38%)
  local copies, waits for them, and re-layouts  28.7 us (9%)
  starting transfers between devices  14.7 us (5%)
  between operations  13.6 us (4%)
  matrix products  9.02 us (3%)
  other arithmetic  6.31 us (2%)
    all_to_all x1, blocking collectives, body(): lax.all_to_all(outgoing, 'req', split_axis=0, concat_axis=0, tiled=True)  111 us
    psum x1, waiting for transfers between devices, body(): projected = lax.psum(partial_value, 'tp')  53.9 us
    all_gather x1, waiting for transfers between devices, body(): lax.all_gather(hidden, 'tp', axis=1, tiled=True)  38.7 us
    all_to_all x1, waiting for transfers between devices, body(): lax.all_to_all(expert_out, 'req', split_axis=0, concat_axis=0, tiled=True)  30.2 us
    all_to_all x1, starting transfers between devices, body(): lax.all_to_all(expert_out, 'req', split_axis=0, concat_axis=0, tiled=True)  14.6 us
    psum x1, blocking collectives, body(): square_total = lax.psum(square_part, 'tp')  9.8 us
  transfers between devices with their start and end apart: 3, of which 3 were waited for; matrix products, arithmetic and copies ran while one was open for 2% of the time, Pallas kernels for 0%

commit v1 on v0

--- a/solution.py
+++ b/solution.py
@@ -36,10 +36,17 @@
     gate_act = jnp.dot(expert_rows, gate_local, preferred_element_type=jnp.float32)
     up_act = jnp.dot(expert_rows, up_local, preferred_element_type=jnp.float32)
     hidden = (jax.nn.silu(gate_act) * up_act).astype(jnp.bfloat16)
+    use_tiles_now = lambda inp, peer_axis: jnp.concatenate(
+        lax.all_to_all(
+            jnp.stack(lax.axis_size(peer_axis) * [inp]),
+            concat_axis=0,
+            axis_name=peer_axis,
+            split_axis=0,
+        ),
+        axis=1,
+    )
     expert_out = jnp.dot(
-        lax.all_gather(hidden, "tp", axis=1, tiled=True),
-        down_local,
-        preferred_element_type=jnp.float32,
+        use_tiles_now(hidden, "tp"), down_local, preferred_element_type=jnp.float32
     )
     expert_out = expert_out.astype(jnp.bfloat16).reshape(slot_count, capacity, down_local.shape[1])
     returned = lax.all_to_all(expert_out, "req", split_axis=0, concat_axis=0, tiled=True)

time: 317 us -> 302 us (0.953)
  waiting for transfers between devices: 123 us -> 84.2 us
  blocking collectives: 121 us -> 143 us
  starting transfers between devices: 14.7 us -> 18.1 us
    all_gather x1 -> x0, waiting for transfers between devices: 38.7 us -> none  [body(): lax.all_gather(hidden, 'tp', axis=1, tiled=True)]
    all_to_all x0 -> x1, blocking collectives: none -> 23.2 us  [body(): lax.all_to_all(jnp.stack(lax.axis_size(peer_axis) * [inp]), concat_axis=0...]
    all_to_all x1, starting transfers between devices: 14.6 us -> 18.1 us  [body(): lax.all_to_all(expert_out, 'req', split_axis=0, concat_axis=0, tiled=True)]
  transfers between devices with their start and end apart: 3 -> 2, of which waited for: 3 -> 2; matrix products, arithmetic and copies ran while one was open for 2% -> 2% of each run, Pallas kernels for 0% -> 0%
where the time goes in v1:
time: 302 us; the launch traced here: 301 us
  blocking collectives  143 us (47%)
  waiting for transfers between devices  84.2 us (28%)
  local copies, waits for them, and re-layouts  29 us (10%)
  starting transfers between devices  18.1 us (6%)
  between operations  13.6 us (5%)
  matrix products  6.61 us (2%)
  other arithmetic  6.31 us (2%)
    all_to_all x1, blocking collectives, body(): lax.all_to_all(outgoing, 'req', split_axis=0, concat_axis=0, tiled=True)  111 us
    psum x1, waiting for transfers between devices, body(): projected = lax.psum(partial_value, 'tp')  53.9 us
    all_to_all x1, waiting for transfers between devices, body(): lax.all_to_all(expert_out, 'req', split_axis=0, concat_axis=0, tiled=True)  30.2 us
    all_to_all x1, blocking collectives, body(): lax.all_to_all(jnp.stack(lax.axis_size(peer_axis) * [inp]), concat_axis=0...  23.2 us
    all_to_all x1, starting transfers between devices, body(): lax.all_to_all(expert_out, 'req', split_axis=0, concat_axis=0, tiled=True)  18.1 us
    psum x1, blocking collectives, body(): square_total = lax.psum(square_part, 'tp')  8.9 us
    reshape x1, local copies, waits for them, and re-layouts, body(): expert_rows = incoming.reshape(slot_count * capacity, full_width)  6.34 us
    reshape x1, local copies, waits for them, and re-layouts, body(): projected.astype(jnp.bfloat16)[source_row]  6.25 us
  transfers between devices with their start and end apart: 2, of which 2 were waited for; matrix products, arithmetic and copies ran while one was open for 2% of the time, Pallas kernels for 0%

profile of v1, /device:TPU:8, one launch (start us, length us, event | category | flops | bytes accessed | tf_op | source)
XLA Modules:
  0.0 300.9 jit_solution(10026098008700047942)
XLA Ops:
  6.5 0.0 copy-start
  6.5 0.0 copy-start.3
  6.5 0.0 all-reduce.2.cloned.1.call-start
  6.5 1.6 copy-done
  8.1 1.3 fusion.12
  9.4 0.9 add_dynamic-update-slice_fusion
  10.3 0.0 copy-start.2
  10.3 0.8 copy-done.2
  11.1 0.0 all-reduce.2.cloned.1.call-update
  11.1 0.0 copy-done.3
  11.1 0.1 copy.12
  11.2 0.1 eq.29
  11.4 0.1 eq.25
  11.5 0.1 copy.14
  11.6 0.2 fusion.5
  11.9 0.1 add_add_fusion
  12.0 0.1 copy.11
  12.1 0.1 mul.61
  12.2 0.1 reshape.106
  12.4 0.2 fusion.7
  12.6 2.9 scatter_custom_fusion
  15.6 53.9 %all-reduce.2.cloned.1.call-done = f32[64,2048]{1,0:T(8,128)} async-done(((f32[64,2048]{1,0:T(8,128)}), f32[64,2048]{1,0:T(8,128)}) %all-reduce.2.cloned.1.call-update) | async-done | bytes 524304 | tf_op jit(solution)/shard_map/psum | solution.py:31
  69.5 1.1 convert_element_type.27
  70.6 4.3 %gather_fusion = bf16[768,2048]{1,0:T(8,128)(2,1)} fusion(bf16[64,2048]{1,0:T(8,128)(2,1)S(1)} %convert_element_type.27, s32[1024]{0:T(1024)S(1)} %pad_clamp_fusion.1), kind=kCustom, calls=%fused_computation | custom fusion | bytes 6294528 | tf_op jit(solution)/shard_map/gather | solution.py:33
  74.9 6.3 %reshape.79 = bf16[128,6,2048]{2,1,0:T(8,128)(2,1)} reshape(bf16[768,2048]{1,0:T(8,128)(2,1)} %gather_fusion) | data formatting | bytes 6291456 | tf_op jit(solution)/shard_map/reshape | solution.py:33
  81.1 111.0 %all_to_all.15 = bf16[128,6,2048]{2,1,0:T(8,128)(2,1)} all-to-all(bf16[128,6,2048]{2,1,0:T(8,128)(2,1)} %reshape.79), channel_id=1, replica_groups=mesh['req'=128,'tp'=4] {'req'}, dimensions={0} | all-to-all | bytes 6291456 | tf_op jit(solution)/shard_map/all_to_all | solution.py:34
  192.1 6.3 %reshape.80 = bf16[768,2048]{1,0:T(8,128)(2,1)} reshape(bf16[128,6,2048]{2,1,0:T(8,128)(2,1)} %all_to_all.15) | data formatting | bytes 6291456 | tf_op jit(solution)/shard_map/reshape | solution.py:35
  198.4 0.0 copy-start.1
  198.4 0.0 copy-start.6
  198.4 3.3 %fusion.3 = f32[768,256]{1,0:T(8,128)S(1)} fusion(bf16[768,2048]{1,0:T(8,128)(2,1)} %reshape.80, bf16[1,2048,256]{2,1,0:T(8,128)(2,1)} %param.14), kind=kOutput, calls=%fused_computation.8 | convolution fusion | flops 805306368 | bytes 4980736 | tf_op jit(solution)/shard_map/dot_general | solution.py:36
  201.7 0.0 copy-done.1
  201.8 0.1 copy-done.6
  201.9 1.0 fusion
  202.9 0.2 copy.16
  203.0 0.0 copy-start.7
  203.0 0.1 stack.2
  203.2 23.2 %all_to_all.16 = bf16[4,768,256]{1,2,0:T(8,128)(2,1)S(1)} all-to-all(bf16[4,768,256]{1,2,0:T(8,128)(2,1)S(1)} %stack.2), channel_id=1, replica_groups=mesh['req'=128,'tp'=4] {'tp'}, dimensions={0} | all-to-all | bytes 3145728 | tf_op jit(solution)/shard_map/all_to_all | solution.py:40
  226.4 0.0 copy-done.7
  226.4 1.0 convolution_convert_fusion
  227.4 0.0 copy-start.4
  227.4 1.3 reshape.83
  228.7 18.1 %all-to-all-start.2 = ((bf16[128,6,512]{2,1,0:T(8,128)(2,1)}), bf16[128,6,512]{2,1,0:T(8,128)(2,1)}, u32[]{:S(2)}, u32[]{:S(2)}) async-start(bf16[128,6,512]{2,1,0:T(8,128)(2,1)} %reshape.83), calls=%async_computation.2 | async-start | bytes 2097152 | tf_op jit(solution)/shard_map/all_to_all | solution.py:52
  246.8 0.0 copy-done.4
  246.8 0.7 copy.17
  247.5 30.2 %all-to-all-done.2 = bf16[128,6,512]{2,1,0:T(8,128)(2,1)} async-done(((bf16[128,6,512]{2,1,0:T(8,128)(2,1)}), bf16[128,6,512]{2,1,0:T(8,128)(2,1)}, u32[]{:S(2)}, u32[]{:S(2)}) %all-to-all-start.2) | async-done | bytes 786464 | tf_op jit(solution)/shard_map/all_to_all | solution.py:52
  277.8 1.4 reshape.84
  279.1 0.0 copy-start.5
  279.2 2.1 gather_fusion.1
  281.2 0.1 reshape.85
  281.3 1.1 multiply_reduce_fusion
  282.5 1.0 multiply_reduce_fusion.1
  283.5 8.9 %psum.15 = f32[64]{0:T(128)S(1)} all-reduce(f32[64]{0:T(128)S(1)} %multiply_reduce_fusion.1), channel_id=1, replica_groups=mesh['req'=128,'tp'=4] {'tp'}, use_global_device_ids=true, to_apply=%region_7.8 | all-reduce | flops 64 | bytes 512 | tf_op jit(solution)/shard_map/psum | solution.py:58
  292.4 0.0 copy-done.5
  292.4 1.6 multiply_convert_fusion
  (10 shorter events, 0.1 us)
Async XLA Ops:
  6.5 1.6 copy-start
  6.5 4.6 %copy-start.3 = (s32[64,6]{0,1:T(8,128)S(1)}, s32[64,6]{0,1:T(8,128)}, u32[]{:S(2)}) copy-start(s32[64,6]{0,1:T(8,128)} %param.12) | copy-start | bytes 4612
  6.5 63.0 %all-reduce.2.cloned.1.call-start = ((), (), s32[]{:S(2)}) async-start(), calls=%async_computation.3 | async-start | bytes 1048576 | tf_op jit(solution)/shard_map/psum | solution.py:31
  10.3 0.8 copy-start.2
  198.4 3.3 %copy-start.1 = (bf16[768,2048]{1,0:T(8,128)(2,1)S(1)}, bf16[768,2048]{1,0:T(8,128)(2,1)}, u32[]{:S(2)}) copy-start(bf16[768,2048]{1,0:T(8,128)(2,1)} %reshape.80) | copy-start | bytes 9437188
  198.4 3.4 %copy-start.6 = (bf16[1,2048,256]{2,1,0:T(8,128)(2,1)S(1)}, bf16[1,2048,256]{2,1,0:T(8,128)(2,1)}, u32[]{:S(2)}) copy-start(bf16[1,2048,256]{2,1,0:T(8,128)(2,1)} %param.15) | copy-start | bytes 3145732
  203.0 23.3 %copy-start.7 = (bf16[1,1024,512]{2,1,0:T(8,128)(2,1)S(1)}, bf16[1,1024,512]{2,1,0:T(8,128)(2,1)}, u32[]{:S(2)}) copy-start(bf16[1,1024,512]{2,1,0:T(8,128)(2,1)} %param.16) | copy-start | bytes 3145732
  227.4 19.4 %copy-start.4 = (f32[64,6]{0,1:T(8,128)S(1)}, f32[64,6]{0,1:T(8,128)}, u32[]{:S(2)}) copy-start(f32[64,6]{0,1:T(8,128)} %param.13) | copy-start | bytes 4612
  228.7 49.1 %all-to-all-start.2 = ((bf16[128,6,512]{2,1,0:T(8,128)(2,1)}), bf16[128,6,512]{2,1,0:T(8,128)(2,1)}, u32[]{:S(2)}, u32[]{:S(2)}) async-start(bf16[128,6,512]{2,1,0:T(8,128)(2,1)} %reshape.83), calls=%async_computation.2 | async-start | bytes 2097152 | tf_op jit(solution)/shard_map/all_to_all | solution.py:52
  279.1 13.3 %copy-start.5 = (f32[512]{0:T(512)S(1)}, f32[512]{0:T(512)}, u32[]{:S(2)}) copy-start(f32[512]{0:T(512)} %param.17) | copy-start | bytes 6148
Sparse Core Ops, SparseCore 0:
  11.3 58.2 all-reduce.1
